TPU v7x, 32 devices: a whole 2x2x4 slice. The times are simulated.
32 devices in a mesh: row: 4 (over y, x), col: 8 (over z, core).
Axes of the slice: x: 2, y: 2, z: 4, core: 2. Of those that a mesh axis runs over, the one named last changes fastest.
Arguments:
- pixels_tokens: bfloat16 [4, 2304, 5120], P(None, 'col', 'row'), may hold values from -12 to 12, as said below
- ln_gain: float32 [5120], replicated, may hold values from 0.1 to 1.9
- ln_bias: float32 [5120], replicated, may hold values from -3 to 3
- w_qkv: bfloat16 [5120, 6144], P('col', 'row'), may hold values from -1 to 1, as said below
- w_out: bfloat16 [2048, 5120], P('col', 'row'), may hold values from -0.125 to 0.125
Outputs:
- block_out: bfloat16 [4, 2304, 5120], P(None, 'col', 'row')
Inputs may be any that keep to these rules, and one draw needn't show every extreme that they name: `pixels_tokens`: activations of order one. `w_qkv`: projection entries scaled by the width.
All inputs are finite; a program needn't handle non-finite values.
Results may differ from a plain program's by a relative error of at most 0.012.
The roundings to bfloat16 on the way count: a program that leaves them out, or rounds other values in their place, can miss the bound.
Values may be sent and summed in bfloat16 or wider, within the bound.
No kernel may reach another device: no remote copies, remote signals or barrier semaphores. Data moves between devices by JAX's collectives and lax.ppermute only.
A program may use at most 128 MiB of HBM per device.

v0:
```python
import jax
import jax.numpy as jnp
from jax import lax
from jax.sharding import PartitionSpec as P

HDIM = 128


def layer_norm(values, ln_gain, ln_bias):
    floats = values.astype(jnp.float32)
    center = jnp.mean(floats, axis=-1, keepdims=True)
    spread = jnp.mean((floats - center) * (floats - center), axis=-1, keepdims=True)
    return ((floats - center) * lax.rsqrt(spread + 1e-06) * ln_gain + ln_bias).astype(jnp.bfloat16)


def attend_item(item):
    width = item.shape[1] // 3
    query = item[:, :width]
    keys = item[:, width : 2 * width]
    values = item[:, 2 * width :]
    blocks = query.reshape(4, item.shape[0] // 4, width)

    def one_block(rows):
        scores = jnp.einsum(
            "qd,kd->qk", rows, keys, preferred_element_type=jnp.float32
        ) * width ** (-0.5)
        peak = jnp.max(scores, axis=-1, keepdims=True)
        expo = jnp.exp(scores - peak)
        weights = (expo / jnp.sum(expo, axis=-1, keepdims=True)).astype(jnp.bfloat16)
        return jnp.dot(weights, values, preferred_element_type=jnp.float32).astype(jnp.bfloat16)

    return lax.map(one_block, blocks).reshape(item.shape[0], width)


def local(pixels_tokens, ln_gain, ln_bias, w_qkv, w_out):
    images, seq_col, width_row = pixels_tokens.shape
    col_count = lax.axis_size("col")
    per_head = 3 * HDIM
    head_row = w_qkv.shape[1] // per_head
    items = images * head_row // col_count
    whole = lax.all_gather(pixels_tokens, "row", axis=2, tiled=True)
    normed = layer_norm(whole, ln_gain, ln_bias).reshape(images * seq_col, whole.shape[2])
    columns = normed
    qkv = jnp.dot(
        columns,
        lax.all_gather(w_qkv, "col", axis=0, tiled=True),
        preferred_element_type=jnp.float32,
    ).astype(jnp.bfloat16)
    outgoing = qkv.reshape(images, seq_col, head_row, per_head).transpose(0, 2, 1, 3)
    outgoing = outgoing.reshape(col_count, items, seq_col, per_head).transpose(1, 0, 2, 3)
    received = lax.all_to_all(outgoing, "col", split_axis=1, concat_axis=2, tiled=True)
    count = received.shape[0]
    heads_out = lax.map(attend_item, received.reshape(count, -1, per_head))
    back_send = heads_out.reshape(items, col_count, seq_col, HDIM)
    returned = lax.all_to_all(back_send, "col", split_axis=1, concat_axis=0, tiled=True)
    mixed = (
        returned.reshape(images, head_row, seq_col, HDIM)
        .transpose(0, 2, 1, 3)
        .reshape(images, seq_col, head_row * HDIM)
    )
    gathered = lax.all_gather(mixed, "row", axis=2, tiled=True)
    flat_heads = gathered.reshape(images * seq_col, gathered.shape[2])
    columns = flat_heads
    projected = jnp.dot(
        columns,
        lax.all_gather(w_out, "col", axis=0, tiled=True),
        preferred_element_type=jnp.float32,
    )
    summed = pixels_tokens.astype(jnp.float32) + projected.reshape(images, seq_col, width_row)
    return summed.astype(jnp.bfloat16)


def solution(mesh):
    in_specs = (P(None, "col", "row"), P(), P(), P("col", "row"), P("col", "row"))
    out_specs = P(None, "col", "row")
    return jax.shard_map(local, mesh=mesh, in_specs=in_specs, out_specs=out_specs, check_vma=False)
```

profile of v0, /device:TPU:0, one launch (start us, length us, event | category | flops | bytes accessed | tf_op | source)
XLA Modules:
  0.0 570.9 jit_solution(7235709859060408799)
XLA Ops:
  6.5 0.7 all-gather.5.cloned.1.call-update
  8.0 119.8 %all-gather.5.cloned.1.call-done = bf16[4,288,5120]{2,1,0:T(8,128)(2,1)} async-done(((bf16[4,288,1280]{2,1,0:T(8,128)(2,1)}), bf16[4,288,5120]{2,1,0:T(8,128)(2,1)}) %all-gather.5.cloned.1.call-update) | async-done | bytes 11796496 | tf_op jit(solution)/shard_map/all_gather | solution.py:41
  127.8 6.0 %convert_reduce_fusion = f32[4,288]{1,0:T(4,128)S(1)} fusion(bf16[4,288,5120]{2,1,0:T(8,128)(2,1)} %all-gather.5.cloned.1.call-done), kind=kLoop, calls=%fused_computation.14 | loop fusion | flops 11795328 | bytes 11801088 | tf_op jit(solution)/shard_map/reduce_sum | solution.py:11
  133.8 8.6 %fusion.10 = f32[4,288]{1,0:T(4,128)S(1)} fusion(bf16[4,288,5120]{2,1,0:T(8,128)(2,1)} %all-gather.5.cloned.1.call-done, f32[4,288]{1,0:T(4,128)S(1)} %broadcast_multiply_fusion), kind=kLoop, calls=%fused_computation.17 | loop fusion | flops 23591808 | bytes 11805696 | tf_op jit(solution)/shard_map/reduce_sum | solution.py:12
  142.5 12.3 %fusion.13 = bf16[4,288,5120]{2,1,0:T(8,128)(2,1)} fusion(bf16[4,288,5120]{2,1,0:T(8,128)(2,1)} %all-gather.5.cloned.1.call-done, f32[5120]{0:T(1024)S(1)} %copy-done.3, f32[5120]{0:T(1024)S(1)} %copy-done.4, f32[4,288]{1,0:T(4,128)S(1)} %add_rsqrt_fusion, f32[4,288]{1,0:T(4,128)S(1)} %broadcast_multiply_fusion), kind=kLoop, calls=%fused_computation.20 | loop fusion | flops 35389440 | bytes 23643136 | tf_op jit(solution)/shard_map/convert_element_type | solution.py:13
  154.8 117.2 %all-gather.7.cloned.1.call-done = bf16[5120,1536]{1,0:T(8,128)(2,1)} async-done(((bf16[640,1536]{1,0:T(8,128)(2,1)}), bf16[5120,1536]{1,0:T(8,128)(2,1)}) %all-gather.7.cloned.1.call-update) | async-done | bytes 15728656 | tf_op jit(solution)/shard_map/all_gather | solution.py:46
  271.9 25.9 %convolution_convert_fusion = bf16[1152,1536]{1,0:T(8,128)(2,1)} fusion(bf16[1152,5120]{1,0:T(8,128)(2,1)} %bitcast.61, bf16[5120,1536]{1,0:T(8,128)(2,1)} %all-gather.7.cloned.1.call-done), kind=kOutput, calls=%fused_computation.21 | convolution fusion | flops 18121162752 | bytes 31064064 | tf_op jit(solution)/shard_map/dot_general | solution.py:44
  297.9 5.8 %reshape.52 = bf16[4,288,4,384]{3,2,1,0:T(4,128)(2,1)S(1)} reshape(bf16[1152,1536]{1,0:T(8,128)(2,1)} %convolution_convert_fusion) | data formatting | bytes 7077888 | tf_op jit(solution)/shard_map/reshape | solution.py:49
  303.7 2.3 copy.12
  306.0 3.7 all-to-all-start
  310.6 121.0 %all-to-all-done = bf16[2,8,288,384]{3,2,0,1:T(8,128)(2,1)S(1)} async-done(((bf16[2,8,288,384]{3,2,0,1:T(8,128)(2,1)}), bf16[2,8,288,384]{3,2,0,1:T(8,128)(2,1)S(1)}, u32[]{:S(2)}, u32[]{:S(2)}) %all-to-all-start) | async-done | bytes 3538976 | tf_op jit(solution)/shard_map/all_to_all | solution.py:51
  431.7 2.2 copy.13
  433.8 29.4 %while.21 = (s32[]{:T(128)}, bf16[2,2304,128]{2,1,0:T(8,128)(2,1)}, bf16[2,2304,384]{2,1,0:T(8,128)(2,1)}, s32[]{:T(128)}, s32[]{:T(128)}, /*index=5*/s32[]{:T(128)}) while((s32[]{:T(128)}, bf16[2,2304,128]{2,1,0:T(8,128)(2,1)}, bf16[2,2304,384]{2,1,0:T(8,128)(2,1)}, s32[]{:T(128)}, s32[]{:T(128)}, /*index=5*/s32[]{:T(128)}) %tuple.44), condition=%wide.region_7.8_spmd, body=%wide.region_2.7_spmd.sunk | while | flops 688839552 | bytes 35109896 | solution.py:53
  433.8 1.7 dynamic-slice_bitcast_fusion.2
  435.8 11.6 %while.22 = (s32[]{:T(128)}, bf16[4,576,128]{2,1,0:T(8,128)(2,1)S(1)}, bf16[4,576,128]{2,1,0:T(8,128)(2,1)S(1)}, bf16[2304,128]{1,0:T(8,128)(2,1)S(1)}, bf16[2304,128]{1,0:T(8,128)(2,1)S(1)}, /*index=5*/s32[]{:T(128)}) while((s32[]{:T(128)}, bf16[4,576,128]{2,1,0:T(8,128)(2,1)S(1)}, bf16[4,576,128]{2,1,0:T(8,128)(2,1)S(1)}, ...), condition=%wide.region_6.6_spmd, body=%wide.region_3.5_spmd.sunk | while | flops 688839552 | bytes 17414988 | solution.py:32
  435.8 0.9 fusion.34
  436.8 0.9 fusion.35
  437.7 1.1 fusion.36
  438.7 0.9 fusion.34
  439.7 0.9 fusion.35
  440.6 1.1 fusion.36
  441.6 0.9 fusion.34
  442.6 0.9 fusion.35
  443.5 1.1 fusion.36
  444.5 0.9 fusion.34
  445.5 0.9 fusion.35
  446.4 1.1 fusion.36
  447.5 1.0 copy-done.2
  448.5 1.7 dynamic-slice_bitcast_fusion.2
  450.5 11.6 %while.22 = (s32[]{:T(128)}, bf16[4,576,128]{2,1,0:T(8,128)(2,1)S(1)}, bf16[4,576,128]{2,1,0:T(8,128)(2,1)S(1)}, bf16[2304,128]{1,0:T(8,128)(2,1)S(1)}, bf16[2304,128]{1,0:T(8,128)(2,1)S(1)}, /*index=5*/s32[]{:T(128)}) while((s32[]{:T(128)}, bf16[4,576,128]{2,1,0:T(8,128)(2,1)S(1)}, bf16[4,576,128]{2,1,0:T(8,128)(2,1)S(1)}, ...), condition=%wide.region_6.6_spmd, body=%wide.region_3.5_spmd.sunk | while | flops 688839552 | bytes 17414988 | solution.py:32
  450.5 0.9 fusion.34
  451.5 0.9 fusion.35
  452.4 1.1 fusion.36
  453.4 0.9 fusion.34
  454.4 0.9 fusion.35
  455.3 1.1 fusion.36
  456.3 0.9 fusion.34
  457.3 0.9 fusion.35
  458.2 1.1 fusion.36
  459.2 0.9 fusion.34
  460.2 0.9 fusion.35
  461.1 1.1 fusion.36
  462.2 1.0 copy-done.2
  463.2 1.5 copy.14
  464.8 31.8 %all_to_all.24 = bf16[2,8,288,128]{3,2,0,1:T(8,128)(2,1)S(1)} all-to-all(bf16[2,8,288,128]{3,2,0,1:T(8,128)(2,1)S(1)} %copy.14), channel_id=1, replica_groups=mesh['row'=4,'col'=8] {'col'}, dimensions={1} | all-to-all | bytes 2359296 | tf_op jit(solution)/shard_map/all_to_all | solution.py:55
  496.5 1.2 copy.18
  497.8 55.8 %all-gather.9.cloned.1.call-done = bf16[4,288,2048]{2,1,0:T(8,128)(2,1)} async-done(((bf16[4,288,512]{2,1,0:T(8,128)(2,1)}), bf16[4,288,2048]{2,1,0:T(8,128)(2,1)}) %all-gather.9.cloned.1.call-update) | async-done | bytes 4718608 | tf_op jit(solution)/shard_map/all_gather | solution.py:61
  553.6 10.8 %add_convert_fusion = bf16[4,288,1280]{2,1,0:T(8,128)(2,1)} fusion(bf16[4,288,1280]{2,1,0:T(8,128)(2,1)S(1)} %copy-done, bf16[4,288,2048]{2,1,0:T(8,128)(2,1)} %all-gather.9.cloned.1.call-done, bf16[2048,1280]{1,0:T(8,128)(2,1)} %all-gather.11.cloned.1.call-done), kind=kOutput, calls=%fused_computation.22 | convolution fusion | flops 6044221440 | bytes 15859712 | tf_op jit(solution)/shard_map/dot_general | solution.py:64
  (29 shorter events, 2.5 us)
Async XLA Ops:
  6.5 121.2 %all-gather.5.cloned.1.call-start = ((), (), s32[]{:S(2)}) async-start(), calls=%async_computation.2 | async-start | bytes 14745600 | tf_op jit(solution)/shard_map/all_gather | solution.py:41
  7.3 264.7 %all-gather.7.cloned.1.call-start = ((), (), s32[]{:S(2)}) async-start(), calls=%async_computation.3 | async-start | bytes 17694720 | tf_op jit(solution)/shard_map/all_gather | solution.py:46
  133.8 8.7 %copy-start.3 = (f32[5120]{0:T(1024)S(1)}, f32[5120]{0:T(1024)}, u32[]{:S(2)}) copy-start(f32[5120]{0:T(1024)} %param.11) | copy-start | bytes 61444
  133.8 8.7 %copy-start.4 = (f32[5120]{0:T(1024)S(1)}, f32[5120]{0:T(1024)}, u32[]{:S(2)}) copy-start(f32[5120]{0:T(1024)} %param.10) | copy-start | bytes 61444
  306.0 125.7 %all-to-all-start = ((bf16[2,8,288,384]{3,2,0,1:T(8,128)(2,1)}), bf16[2,8,288,384]{3,2,0,1:T(8,128)(2,1)S(1)}, u32[]{:S(2)}, u32[]{:S(2)}) async-start(bf16[2,8,288,384]{3,2,0,1:T(8,128)(2,1)} %bitcast.60), calls=%async_computation | async-start | bytes 7077888 | tf_op jit(solution)/shard_map/all_to_all | solution.py:51
  309.7 188.1 %all-gather.11.cloned.1.call-start = ((), (), s32[]{:S(2)}) async-start(), calls=%async_computation.5 | async-start | bytes 5898240 | tf_op jit(solution)/shard_map/all_gather | solution.py:66
  310.4 243.2 %all-gather.9.cloned.1.call-start = ((), (), s32[]{:S(2)}) async-start(), calls=%async_computation.4 | async-start | bytes 5898240 | tf_op jit(solution)/shard_map/all_gather | solution.py:61
  435.8 11.6 %copy-start.1 = (bf16[2,2304,128]{2,1,0:T(8,128)(2,1)S(1)}, bf16[2,2304,128]{2,1,0:T(8,128)(2,1)}, u32[]{:S(2)}) copy-start(bf16[2,2304,128]{2,1,0:T(8,128)(2,1)} %get-tuple-element.169) | copy-start | bytes 3538948 | tf_op jit(solution)/shard_map/while
  447.5 1.0 copy-start.2
  450.5 11.6 %copy-start.1 = (bf16[2,2304,128]{2,1,0:T(8,128)(2,1)S(1)}, bf16[2,2304,128]{2,1,0:T(8,128)(2,1)}, u32[]{:S(2)}) copy-start(bf16[2,2304,128]{2,1,0:T(8,128)(2,1)} %get-tuple-element.169) | copy-start | bytes 3538948 | tf_op jit(solution)/shard_map/while
  462.2 1.0 copy-start.2
  463.2 90.3 %copy-start = (bf16[4,288,1280]{2,1,0:T(8,128)(2,1)S(1)}, bf16[4,288,1280]{2,1,0:T(8,128)(2,1)}, u32[]{:S(2)}) copy-start(bf16[4,288,1280]{2,1,0:T(8,128)(2,1)} %param.9) | copy-start | bytes 8847364
Sparse Core Ops, SparseCore 0:
  9.2 118.5 all-gather.4
  129.4 142.4 all-gather.6
  312.1 110.7 all-gather.10
  497.9 55.6 all-gather.8
where the time goes:
time: 571 us
  waiting for transfers between devices  416 us (73%)
  matrix products  52.8 us (9%)
  other arithmetic  33.9 us (6%)
  blocking collectives  31.8 us (6%)
  local copies, waits for them, and re-layouts  19.1 us (3%)
  between operations  13.2 us (2%)
    all_to_all x1, waiting for transfers between devices, local(): lax.all_to_all(outgoing, 'col', split_axis=1, concat_axis=2, tiled=True)  121 us
    all_gather x1, waiting for transfers between devices, local(): whole = lax.all_gather(pixels_tokens, 'row', axis=2, tiled=True)  120 us
    all_gather x1, waiting for transfers between devices, local(): lax.all_gather(w_qkv, 'col', axis=0, tiled=True)  117 us
    all_gather x1, waiting for transfers between devices, local(): gathered = lax.all_gather(mixed, 'row', axis=2, tiled=True)  55.8 us
    all_to_all x1, blocking collectives, local(): lax.all_to_all(back_send, 'col', split_axis=1, concat_axis=0, tiled=True)  31.8 us
    dot_general x1, matrix products, local(): jnp.dot(columns, lax.all_gather(w_qkv, 'col', axis=0, tiled=True), prefer...  25.9 us
    convert_element_type x1, other arithmetic, layer_norm(): ((floats - center) * lax.rsqrt(spread + 1e-06) * ln_gain + ln_bias).astyp...  12.3 us
  transfers between devices with their start and end apart: 5, of which 4 were waited for; matrix products, arithmetic and copies ran while one was open for 10% of the time, Pallas kernels for 0%

commit v1 on v0

--- a/solution.py
+++ b/solution.py
@@ -48,7 +48,10 @@
     ).astype(jnp.bfloat16)
     outgoing = qkv.reshape(images, seq_col, head_row, per_head).transpose(0, 2, 1, 3)
     outgoing = outgoing.reshape(col_count, items, seq_col, per_head).transpose(1, 0, 2, 3)
-    received = lax.all_to_all(outgoing, "col", split_axis=1, concat_axis=2, tiled=True)
+    received = jnp.concatenate(
+        lax.all_to_all(jnp.stack(jnp.split(outgoing, lax.axis_size("col"), axis=1)), "col", 0, 0),
+        axis=2,
+    )
     count = received.shape[0]
     heads_out = lax.map(attend_item, received.reshape(count, -1, per_head))
     back_send = heads_out.reshape(items, col_count, seq_col, HDIM)

time: 571 us -> 576 us (level)
  no operation moved by 1% of the time
where the time goes in v1:
time: 576 us
  waiting for transfers between devices  416 us (72%)
  matrix products  52.8 us (9%)
  other arithmetic  33.9 us (6%)
  blocking collectives  32 us (6%)
  local copies, waits for them, and re-layouts  23.7 us (4%)
  between operations  13.2 us (2%)
    all_to_all x1, waiting for transfers between devices, local(): lax.all_to_all(jnp.stack(jnp.split(outgoing, lax.axis_size('col'), axis=1...  121 us
    all_gather x1, waiting for transfers between devices, local(): whole = lax.all_gather(pixels_tokens, 'row', axis=2, tiled=True)  120 us
    all_gather x1, waiting for transfers between devices, local(): lax.all_gather(w_qkv, 'col', axis=0, tiled=True)  117 us
    all_gather x1, waiting for transfers between devices, local(): gathered = lax.all_gather(mixed, 'row', axis=2, tiled=True)  55.7 us
    all_to_all x1, blocking collectives, local(): lax.all_to_all(back_send, 'col', split_axis=1, concat_axis=0, tiled=True)  32 us
    dot_general x1, matrix products, local(): jnp.dot(columns, lax.all_gather(w_qkv, 'col', axis=0, tiled=True), prefer...  25.9 us
    convert_element_type x1, other arithmetic, layer_norm(): ((floats - center) * lax.rsqrt(spread + 1e-06) * ln_gain + ln_bias).astyp...  12.3 us
  transfers between devices with their start and end apart: 5, of which 4 were waited for; matrix products, arithmetic and copies ran while one was open for 10% of the time, Pallas kernels for 0%

profile of v1, /device:TPU:0, one launch (start us, length us, event | category | flops | bytes accessed | tf_op | source)
XLA Modules:
  0.0 575.8 jit_solution(10762015638492208365)
XLA Ops:
  8.0 119.8 %all-gather.5.cloned.1.call-done = bf16[4,288,5120]{2,1,0:T(8,128)(2,1)} async-done(((bf16[4,288,1280]{2,1,0:T(8,128)(2,1)}), bf16[4,288,5120]{2,1,0:T(8,128)(2,1)}) %all-gather.5.cloned.1.call-update) | async-done | bytes 11796496 | tf_op jit(solution)/shard_map/all_gather | solution.py:41
  127.8 6.0 %convert_reduce_fusion = f32[4,288]{1,0:T(4,128)S(1)} fusion(bf16[4,288,5120]{2,1,0:T(8,128)(2,1)} %all-gather.5.cloned.1.call-done), kind=kLoop, calls=%fused_computation.14 | loop fusion | flops 11795328 | bytes 11801088 | tf_op jit(solution)/shard_map/reduce_sum | solution.py:11
  133.8 8.6 %fusion.10 = f32[4,288]{1,0:T(4,128)S(1)} fusion(bf16[4,288,5120]{2,1,0:T(8,128)(2,1)} %all-gather.5.cloned.1.call-done, f32[4,288]{1,0:T(4,128)S(1)} %broadcast_multiply_fusion), kind=kLoop, calls=%fused_computation.17 | loop fusion | flops 23591808 | bytes 11805696 | tf_op jit(solution)/shard_map/reduce_sum | solution.py:12
  142.5 12.3 %fusion.13 = bf16[4,288,5120]{2,1,0:T(8,128)(2,1)} fusion(bf16[4,288,5120]{2,1,0:T(8,128)(2,1)} %all-gather.5.cloned.1.call-done, f32[5120]{0:T(1024)S(1)} %copy-done.3, f32[5120]{0:T(1024)S(1)} %copy-done.4, f32[4,288]{1,0:T(4,128)S(1)} %add_rsqrt_fusion, f32[4,288]{1,0:T(4,128)S(1)} %broadcast_multiply_fusion), kind=kLoop, calls=%fused_computation.20 | loop fusion | flops 35389440 | bytes 23643136 | tf_op jit(solution)/shard_map/convert_element_type | solution.py:13
  154.8 117.2 %all-gather.7.cloned.1.call-done = bf16[5120,1536]{1,0:T(8,128)(2,1)} async-done(((bf16[640,1536]{1,0:T(8,128)(2,1)}), bf16[5120,1536]{1,0:T(8,128)(2,1)}) %all-gather.7.cloned.1.call-update) | async-done | bytes 15728656 | tf_op jit(solution)/shard_map/all_gather | solution.py:46
  271.9 25.9 %convolution_convert_fusion = bf16[1152,1536]{1,0:T(8,128)(2,1)} fusion(bf16[1152,5120]{1,0:T(8,128)(2,1)} %bitcast.102, bf16[5120,1536]{1,0:T(8,128)(2,1)} %all-gather.7.cloned.1.call-done), kind=kOutput, calls=%fused_computation.21 | convolution fusion | flops 18121162752 | bytes 31064064 | tf_op jit(solution)/shard_map/dot_general | solution.py:44
  297.9 5.8 %reshape.48 = bf16[4,288,4,384]{3,2,1,0:T(4,128)(2,1)S(1)} reshape(bf16[1152,1536]{1,0:T(8,128)(2,1)} %convolution_convert_fusion) | data formatting | bytes 7077888 | tf_op jit(solution)/shard_map/reshape | solution.py:49
  309.1 0.9 fusion.19
  309.9 0.8 fusion.18
  310.7 3.7 all-to-all-start
  315.4 121.0 %all-to-all-done = bf16[8,2,1,288,384]{4,3,1,2,0:T(8,128)(2,1)S(1)} async-done(((bf16[8,2,1,288,384]{4,3,1,2,0:T(8,128)(2,1)}), bf16[8,2,1,288,384]{4,3,1,2,0:T(8,128)(2,1)S(1)}, u32[]{:S(2)}, u32[]{:S(2)}) %all-to-all-start) | async-done | bytes 3538976 | tf_op jit(solution)/shard_map/all_to_all | solution.py:52
  436.4 2.2 copy.20
  438.6 29.4 %while.21 = (s32[]{:T(128)}, bf16[2,2304,128]{2,1,0:T(8,128)(2,1)}, bf16[2,2304,384]{2,1,0:T(8,128)(2,1)}, s32[]{:T(128)}, s32[]{:T(128)}, /*index=5*/s32[]{:T(128)}) while((s32[]{:T(128)}, bf16[2,2304,128]{2,1,0:T(8,128)(2,1)}, bf16[2,2304,384]{2,1,0:T(8,128)(2,1)}, s32[]{:T(128)}, s32[]{:T(128)}, /*index=5*/s32[]{:T(128)}) %tuple.44), condition=%wide.region_7.8_spmd, body=%wide.region_2.7_spmd.sunk | while | flops 688839552 | bytes 35109896 | solution.py:56
  438.6 1.7 dynamic-slice_bitcast_fusion.2
  440.6 11.6 %while.22 = (s32[]{:T(128)}, bf16[4,576,128]{2,1,0:T(8,128)(2,1)S(1)}, bf16[4,576,128]{2,1,0:T(8,128)(2,1)S(1)}, bf16[2304,128]{1,0:T(8,128)(2,1)S(1)}, bf16[2304,128]{1,0:T(8,128)(2,1)S(1)}, /*index=5*/s32[]{:T(128)}) while((s32[]{:T(128)}, bf16[4,576,128]{2,1,0:T(8,128)(2,1)S(1)}, bf16[4,576,128]{2,1,0:T(8,128)(2,1)S(1)}, ...), condition=%wide.region_6.6_spmd, body=%wide.region_3.5_spmd.sunk | while | flops 688839552 | bytes 17414988 | solution.py:32
  440.6 0.9 fusion.42
  441.6 0.9 fusion.43
  442.4 1.1 fusion.44
  443.5 1.0 fusion.42
  444.5 0.9 fusion.43
  445.3 1.1 fusion.44
  446.4 1.0 fusion.42
  447.4 0.9 fusion.43
  448.2 1.1 fusion.44
  449.3 1.0 fusion.42
  450.3 0.9 fusion.43
  451.1 1.1 fusion.44
  452.3 1.0 copy-done.2
  453.3 1.7 dynamic-slice_bitcast_fusion.2
  455.3 11.6 %while.22 = (s32[]{:T(128)}, bf16[4,576,128]{2,1,0:T(8,128)(2,1)S(1)}, bf16[4,576,128]{2,1,0:T(8,128)(2,1)S(1)}, bf16[2304,128]{1,0:T(8,128)(2,1)S(1)}, bf16[2304,128]{1,0:T(8,128)(2,1)S(1)}, /*index=5*/s32[]{:T(128)}) while((s32[]{:T(128)}, bf16[4,576,128]{2,1,0:T(8,128)(2,1)S(1)}, bf16[4,576,128]{2,1,0:T(8,128)(2,1)S(1)}, ...), condition=%wide.region_6.6_spmd, body=%wide.region_3.5_spmd.sunk | while | flops 688839552 | bytes 17414988 | solution.py:32
  455.3 1.0 fusion.42
  456.3 0.9 fusion.43
  457.2 1.1 fusion.44
  458.2 0.9 fusion.42
  459.2 0.9 fusion.43
  460.0 1.1 fusion.44
  461.1 0.9 fusion.42
  462.1 0.9 fusion.43
  462.9 1.1 fusion.44
  464.0 0.9 fusion.42
  465.0 0.9 fusion.43
  465.8 1.1 fusion.44
  467.0 1.0 copy-done.2
  468.0 1.3 copy.21
  469.4 32.0 %all_to_all.20 = bf16[2,8,288,128]{3,2,0,1:T(8,128)(2,1)S(1)} all-to-all(bf16[2,8,288,128]{3,2,0,1:T(8,128)(2,1)S(1)} %copy.21), channel_id=1, replica_groups=mesh['row'=4,'col'=8] {'col'}, dimensions={1} | all-to-all | bytes 2359296 | tf_op jit(solution)/shard_map/all_to_all | solution.py:58
  501.4 1.2 copy.25
  502.7 55.7 %all-gather.9.cloned.1.call-done = bf16[4,288,2048]{2,1,0:T(8,128)(2,1)} async-done(((bf16[4,288,512]{2,1,0:T(8,128)(2,1)}), bf16[4,288,2048]{2,1,0:T(8,128)(2,1)}) %all-gather.9.cloned.1.call-update) | async-done | bytes 4718608 | tf_op jit(solution)/shard_map/all_gather | solution.py:64
  558.5 10.8 %add_convert_fusion = bf16[4,288,1280]{2,1,0:T(8,128)(2,1)} fusion(bf16[4,288,1280]{2,1,0:T(8,128)(2,1)S(1)} %copy-done, bf16[4,288,2048]{2,1,0:T(8,128)(2,1)} %all-gather.9.cloned.1.call-done, bf16[2048,1280]{1,0:T(8,128)(2,1)} %all-gather.11.cloned.1.call-done), kind=kOutput, calls=%fused_computation.22 | convolution fusion | flops 6044221440 | bytes 15859712 | tf_op jit(solution)/shard_map/dot_general | solution.py:67
  (37 shorter events, 8.6 us)
Async XLA Ops:
  6.5 121.2 %all-gather.5.cloned.1.call-start = ((), (), s32[]{:S(2)}) async-start(), calls=%async_computation.2 | async-start | bytes 14745600 | tf_op jit(solution)/shard_map/all_gather | solution.py:41
  7.3 264.7 %all-gather.7.cloned.1.call-start = ((), (), s32[]{:S(2)}) async-start(), calls=%async_computation.3 | async-start | bytes 17694720 | tf_op jit(solution)/shard_map/all_gather | solution.py:46
  133.8 8.7 %copy-start.3 = (f32[5120]{0:T(1024)S(1)}, f32[5120]{0:T(1024)}, u32[]{:S(2)}) copy-start(f32[5120]{0:T(1024)} %param.11) | copy-start | bytes 61444
  133.8 8.7 %copy-start.4 = (f32[5120]{0:T(1024)S(1)}, f32[5120]{0:T(1024)}, u32[]{:S(2)}) copy-start(f32[5120]{0:T(1024)} %param.10) | copy-start | bytes 61444
  310.7 125.7 %all-to-all-start = ((bf16[8,2,1,288,384]{4,3,1,2,0:T(8,128)(2,1)}), bf16[8,2,1,288,384]{4,3,1,2,0:T(8,128)(2,1)S(1)}, u32[]{:S(2)}, u32[]{:S(2)}) async-start(bf16[8,2,1,288,384]{4,3,1,2,0:T(8,128)(2,1)} %fusion.18), calls=%async_computation | async-start | bytes 7077888 | tf_op jit(solution)/shard_map/all_to_all | solution.py:52
  314.4 188.3 %all-gather.11.cloned.1.call-start = ((), (), s32[]{:S(2)}) async-start(), calls=%async_computation.5 | async-start | bytes 5898240 | tf_op jit(solution)/shard_map/all_gather | solution.py:69
  315.2 243.3 %all-gather.9.cloned.1.call-start = ((), (), s32[]{:S(2)}) async-start(), calls=%async_computation.4 | async-start | bytes 5898240 | tf_op jit(solution)/shard_map/all_gather | solution.py:64
  440.6 11.6 %copy-start.1 = (bf16[2,2304,128]{2,1,0:T(8,128)(2,1)S(1)}, bf16[2,2304,128]{2,1,0:T(8,128)(2,1)}, u32[]{:S(2)}) copy-start(bf16[2,2304,128]{2,1,0:T(8,128)(2,1)} %get-tuple-element.169) | copy-start | bytes 3538948 | tf_op jit(solution)/shard_map/while
  452.3 1.0 copy-start.2
  455.3 11.6 %copy-start.1 = (bf16[2,2304,128]{2,1,0:T(8,128)(2,1)S(1)}, bf16[2,2304,128]{2,1,0:T(8,128)(2,1)}, u32[]{:S(2)}) copy-start(bf16[2,2304,128]{2,1,0:T(8,128)(2,1)} %get-tuple-element.169) | copy-start | bytes 3538948 | tf_op jit(solution)/shard_map/while
  467.0 1.0 copy-start.2
  469.4 89.1 %copy-start = (bf16[4,288,1280]{2,1,0:T(8,128)(2,1)S(1)}, bf16[4,288,1280]{2,1,0:T(8,128)(2,1)}, u32[]{:S(2)}) copy-start(bf16[4,288,1280]{2,1,0:T(8,128)(2,1)} %param.9) | copy-start | bytes 8847364
Sparse Core Ops, SparseCore 0:
  9.2 118.5 all-gather.4
  129.4 142.4 all-gather.6
  316.9 110.7 all-gather.10
  502.8 55.6 all-gather.8
